TPU v7x, 32 devices: a whole 2x2x4 slice. The times are simulated.
32 devices in a mesh: dp: 8 (over y, x, core), tensor: 4 (over z).
Axes of the slice: x: 2, y: 2, z: 4, core: 2. Of those that a mesh axis runs over, the one named last changes fastest.
Arguments:
- layer_input: bfloat16 [16, 768, 768], P('dp', 'tensor'), may hold values from -6 to 6
- word_segments: int32 [16, 256], P('dp'), may hold values from 0 to 13, never falling along the last dimension, each value on 1 to 36 neighbouring positions
- image_order: int32 [16, 14], P('dp'), may hold values from 0 to 13, each once within a row
- cross_qkv: bfloat16 [3, 768, 768], P(None, None, 'tensor'), may hold values from -0.21875 to 0.21875
- cross_out: bfloat16 [768, 768], P('tensor'), may hold values from -0.875 to 0.875
- self_qkv: bfloat16 [2, 3, 768, 768], P(None, None, None, 'tensor'), may hold values from -0.21875 to 0.21875
- self_out: bfloat16 [2, 768, 768], P(None, 'tensor'), may hold values from -0.875 to 0.875
- ffn_up: bfloat16 [2, 768, 3072], P(None, None, 'tensor'), may hold values from -0.21875 to 0.21875
- ffn_down: bfloat16 [2, 3072, 768], P(None, 'tensor'), may hold values from -0.109375 to 0.109375
- norm_gains: float32 [5, 768], replicated, may hold values from 0.5 to 1.5
- norm_biases: float32 [5, 768], replicated, may hold values from -3 to 3
- out_grad: bfloat16 [16, 768, 768], P('dp', 'tensor'), may hold values from -6 to 6
Outputs:
- layer_output: bfloat16 [16, 768, 768], P('dp', 'tensor')
- input_grad: float32 [16, 768, 768], P('dp', 'tensor')
- cross_qkv_grad: float32 [3, 768, 768], P(None, None, 'tensor')
- cross_out_grad: float32 [768, 768], P('tensor')
- self_qkv_grad: float32 [2, 3, 768, 768], P(None, None, None, 'tensor')
- self_out_grad: float32 [2, 768, 768], P(None, 'tensor')
- ffn_up_grad: float32 [2, 768, 3072], P(None, None, 'tensor')
- ffn_down_grad: float32 [2, 3072, 768], P(None, 'tensor')
- norm_gains_grad: float32 [5, 768], replicated
- norm_biases_grad: float32 [5, 768], replicated
Inputs may be any that keep to these rules, and one draw needn't show every extreme that they name: `word_segments`: in each row the ids never fall along the word slots, and each of the 14 captions has 1 to 36 slots. `image_order`: each row names every image once.
All inputs are finite; a program needn't handle non-finite values.
Results may differ from a plain program's by a relative error of at most 0.035.
Values may be sent and summed in bfloat16 or wider, within the bound.
A program may use at most 192 MiB of HBM per device.

v0:
```python
import functools

import jax
import jax.numpy as jnp
from jax import lax
from jax.experimental import pallas as pl
from jax.experimental.pallas import tpu as pltpu
from jax.sharding import PartitionSpec as P

HEAD_DIM = 64
WORDS = 256
CAPTIONS = 14
BOXES = 36
REGIONS = 504
PADS = 8
NORM_EPSILON = 1e-12
BLOCK = 256
BF16 = jnp.bfloat16
F32 = jnp.float32
MESH = pl.DeviceIdType.MESH
CROSS, SELF, UP, DOWN = 0, 1, 2, 3


def dot_nn(left, right):
    return jnp.dot(left, right, preferred_element_type=F32)


def dot_nt(left, right):
    return lax.dot_general(left, right, (((1,), (1,)), ((), ())), preferred_element_type=F32)


def aligned(value, step):
    return pl.multiple_of(value, step)


def layer_kernel(
    x_in,
    og_in,
    codes_in,
    cross_in,
    self_in,
    up_in,
    down_in,
    gains,
    biases,
    y_out,
    dx_out,
    cross_out,
    self_out,
    up_out,
    down_out,
    norm_out,
    wa,
    wf,
    xrow,
    ogrow,
    codes,
    kcode,
    qkv1,
    qkv2,
    ctx_t,
    lse,
    xh,
    rstd,
    sb,
    res,
    acc,
    act,
    gp,
    dzb,
    tt,
    yb,
    dhk_recv,
    kv_acc,
    nrm,
    nrm_recv,
    s2all,
    zall,
    qacc,
    rq,
    r2s,
    r3s,
    r2c,
    r3c,
    send_sems,
    recv_sems,
    local_sems,
    credit,
):
    d = lax.axis_index("dp")
    t = lax.axis_index("tensor")
    c = d % 2
    px = (d // 2) % 2
    py = (d // 4) % 2
    q = px + 2 * py
    d_core = d + 1 - 2 * c
    d_x = d + 2 - 4 * px
    d_y = d + 4 - 8 * py
    holder = t // 2
    d_holder = d - c + holder
    turn = t % 2
    nb = 1 + c
    near = {"x": d_x, "y": d_y, "core": d_core}

    def at(dp_index, tensor_index):
        return {"dp": dp_index, "tensor": tensor_index}

    counter = [0]
    local_counter = [0]
    pending = []

    def new_id(count=1):
        counter[0] += count
        return counter[0] - count

    def remote(src, dst, device, ident, arrival=None):
        return pltpu.make_async_remote_copy(
            src_ref=src,
            dst_ref=dst,
            send_sem=send_sems.at[ident],
            recv_sem=recv_sems.at[ident if arrival is None else arrival],
            device_id=device,
            device_id_type=MESH,
        )

    def send(src, dst, device, ident):
        copy = remote(src, dst, device, ident)
        copy.start()
        pending.append(copy.wait_send)

    def arrive(dst, ident):
        remote(dst, dst, at(d_core, t), ident).wait_recv()

    def local(src, dst):
        copy = pltpu.make_async_copy(src, dst, local_sems.at[local_counter[0]])
        local_counter[0] += 1
        return copy

    def blocks(body):
        def step(i, carry):
            body(i, aligned(i * BLOCK, BLOCK))
            return carry

        lax.fori_loop(0, nb, step, 0)

    def times(count, body):
        def step(i, carry):
            body(i)
            return carry

        lax.fori_loop(0, count, step, 0)

    barrier = pltpu.get_barrier_semaphore()
    partners = [at(d_core, t), at(d_x, t), at(d_y, t)]
    for m in range(1, 4):
        partners.append(at(d, (t + m) % 4))
        partners.append(at(d_core, (t + m) % 4))
    for partner in partners:
        pl.semaphore_signal(barrier, inc=1, device_id=partner, device_id_type=MESH)

    half_rows = aligned(t * 192, 16)
    own_copies = [
        local(cross_in, wa.at[CROSS, :, pl.ds(half_rows, 192), :]),
        local(self_in.at[c], wa.at[SELF, :, pl.ds(half_rows, 192), :]),
        local(down_in.at[c], wf.at[1, t]),
    ]
    up_copies = [
        local(up_in.at[c, pl.ds(0, 512), :], qkv1.at[0]),
        local(up_in.at[c, pl.ds(512, 256), :], qkv1.at[1, pl.ds(0, 256), :]),
    ]
    for copy in own_copies + up_copies:
        copy.start()

    zero_half = jnp.zeros((BLOCK, 768), BF16)

    @pl.when(c == 0)
    def _():
        for ref in (qkv2.at[1], qkv2.at[2], sb, dzb):
            ref[BLOCK:, :] = zero_half
        for k in range(2):
            ctx_t[k, :, BLOCK:] = jnp.zeros((768, BLOCK), BF16)
        tt[0, :, BLOCK:] = jnp.zeros((768, BLOCK), BF16)

    nrm[...] = jnp.zeros_like(nrm)
    pl.semaphore_wait(barrier, len(partners))

    def spread_row(source, row):
        base = new_id(4)
        core_base = new_id(4)
        own = local(source.at[turn], row.at[pl.ds(half_rows, 192), :])

        def each_target(action):
            for r in range(2):
                target = 2 * c + r

                @pl.when(target != t)
                def _():
                    action(
                        remote(
                            source.at[r],
                            row.at[pl.ds(half_rows, 192), :],
                            at(d, target),
                            base + r,
                            base + t,
                        )
                    )

        def each_relay(action):
            @pl.when(holder == c)
            def _():
                for s in range(4):
                    part = row.at[pl.ds(192 * s, 192), :]
                    action(s, part, remote(part, part, at(d_core, t), core_base + s))

        def begin():
            each_target(lambda copy: copy.start())

            @pl.when(holder == c)
            def _():
                own.start()

        def relay():
            def action(s, part, copy):
                @pl.when(t == s)
                def _():
                    own.wait()

                @pl.when(t != s)
                def _():
                    arrive(part, base + s)

                copy.start()

            each_relay(action)

        def finish():
            @pl.when(holder != c)
            def _():
                for s in range(4):
                    arrive(row.at[pl.ds(192 * s, 192), :], core_base + s)

        def close():
            each_target(lambda copy: copy.wait_send())
            each_relay(lambda s, part, copy: copy.wait_send())

        return begin, relay, finish, close

    x_begin, x_relay, x_finish, x_close = spread_row(x_in, xrow)
    og_begin, og_relay, og_finish, og_close = spread_row(og_in, ogrow)
    pending.append(x_close)

    code_ident = new_id()
    code_own = local(codes_in.at[turn], codes)

    @pl.when(holder == c)
    def _():
        code_own.start()
        remote(codes_in.at[turn], codes, at(d_core, t), code_ident).start()

    def share(g, shard, quarter, low, high):
        if g >= UP:
            rows = aligned(quarter * 192 + low * 96, 16)
            return wf.at[g - UP, shard, pl.ds(rows, (high - low) * 96), :]
        rows = aligned(shard * 192 + quarter * 48, 16)
        if g == SELF:
            return wa.at[SELF, pl.ds(2 * low, 2 * (high - low)), pl.ds(rows, 48), :]
        return wa.at[CROSS, pl.ds(2 * c + low, high - low), pl.ds(rows, 48), :]

    def own_share(g):
        if g >= UP:
            rows = pl.ds(aligned(q * 192, 16), 192)
            return wf.at[0, t, rows, :] if g == UP else down_in.at[c, rows, :]
        rows = pl.ds(aligned(q * 48, 16), 48)
        if g == SELF:
            return self_in.at[c, :, rows, :]
        return cross_in.at[pl.ds(2 * c, 2), rows, :]

    qx, qy = (1 - px) + 2 * py, px + 2 * (1 - py)
    qd = (1 - px) + 2 * (1 - py)
    items = [(g, m) for g in (CROSS, SELF, UP, DOWN) for m in range(1, 4)]
    z_base = {g: new_id(4) for g in (CROSS, SELF, UP, DOWN)}
    own_ids = {g: new_id(2) for g in (CROSS, SELF, UP, DOWN)}
    pass_ids = {item: new_id() for item in items}
    x_ids = {item: new_id() for item in items}
    y_ids = {item: new_id() for item in items}
    fx_ids = {item: new_id() for item in items}
    fy_ids = {item: new_id() for item in items}
    core_ids = {m: new_id() for m in range(1, 4)}
    arrivals = {
        1: t + 1 - 2 * (t % 2),
        2: 2 - t // 2,
        3: 3 - 3 * (t // 2),
    }

    def z_way(g, way):
        exists = t > 0 if way == 0 else t < 3
        target = t - 1 + 2 * way

        def copy():
            return remote(
                own_share(g),
                share(g, t, q, 0, 2),
                at(d, target),
                own_ids[g] + way,
                z_base[g] + t,
            )

        @pl.when(exists)
        def _():
            copy().start()

        def close():
            @pl.when(exists)
            def _():
                copy().wait_send()

        pending.append(close)

    def z_own(g):
        for way in range(2):
            z_way(g, way)

    def first(item):
        g, m = item
        shard = arrivals[m]
        piece = share(g, shard, q, 0, 2)
        arrive(piece, z_base[g] + shard)
        inner = jnp.logical_and(t > 0, t < 3)
        target = jnp.where(shard < t, t + 1, t - 1)

        def copy():
            return remote(piece, piece, at(d, target), pass_ids[item], z_base[g] + shard)

        @pl.when(inner)
        def _():
            copy().start()

        def close():
            @pl.when(inner)
            def _():
                copy().wait_send()

        pending.append(close)
        send(piece, piece, at(d_x, t), x_ids[item])
        send(piece, piece, at(d_y, t), y_ids[item])
        if m == 1 and g < DOWN:
            z_own(g + 1)
        if g == CROSS and m == 1:
            x_begin()
        if item == (DOWN, 1):
            og_begin()

    def second(item):
        g, m = item
        shard = arrivals[m]
        arrive(share(g, shard, qx, 0, 2), x_ids[item])
        low = share(g, shard, qx, 0, 1)
        send(low, low, at(d_y, t), fy_ids[item])
        arrive(share(g, shard, qy, 0, 2), y_ids[item])
        high = share(g, shard, qy, 1, 2)
        send(high, high, at(d_x, t), fx_ids[item])

    def third(item):
        g, m = item
        shard = arrivals[m]
        arrive(share(g, shard, qd, 0, 1), fy_ids[item])
        arrive(share(g, shard, qd, 1, 2), fx_ids[item])
        if g == CROSS:
            rows = pl.ds(aligned(shard * 192, 16), 192)
            whole = wa.at[CROSS, pl.ds(2 * c, 2), rows, :]
            send(whole, whole, at(d_core, t), core_ids[m])

    def last(m):
        shard = arrivals[m]
        rows = pl.ds(aligned(shard * 192, 16), 192)
        arrive(wa.at[CROSS, pl.ds(2 * (1 - c), 2), rows, :], core_ids[m])

    z_own(CROSS)
    for copy in up_copies:
        copy.wait()
    wf[0, t, :, 0:512] = jnp.transpose(qkv1[0])
    wf[0, t, :, 512:768] = jnp.transpose(qkv1[1, 0:256, :])

    steps = []
    position = {}
    for k in range(len(items) + 2):
        if k < len(items):
            steps.append(functools.partial(first, items[k]))
        if 0 <= k - 1 < len(items):
            steps.append(functools.partial(second, items[k - 1]))
        if 0 <= k - 2 < len(items):
            steps.append(functools.partial(third, items[k - 2]))
            position[items[k - 2]] = len(steps)
    done = [0]

    def advance(upto):
        while done[0] < min(upto, len(steps)):
            steps[done[0]]()
            done[0] += 1

    advance(position[(CROSS, 2)])
    x_relay()
    x_finish()

    @pl.when(holder == c)
    def _():
        code_own.wait()
        remote(codes_in.at[turn], codes, at(d_core, t), code_ident).wait_send()

    @pl.when(holder != c)
    def _():
        arrive(codes, code_ident)

    def as_column(row):
        return jnp.transpose(jnp.broadcast_to(row, (128, BLOCK)))

    own_base = aligned(c * BLOCK, BLOCK)
    other_base = aligned((1 - c) * BLOCK, BLOCK)
    kcode[0, :BLOCK, :] = as_column(codes[0:1, pl.ds(other_base, BLOCK)])
    kcode[0, BLOCK:, :] = as_column(codes[pl.ds(c, 1), 512:768])
    kcode[1, :BLOCK, :] = as_column(codes[2:3, pl.ds(own_base, BLOCK)])
    kcode[1, BLOCK:, :] = as_column(codes[pl.ds(3 - c, 1), 512:768])

    lane = lax.broadcasted_iota(jnp.int32, (1, 128), 1)
    head_lanes = [
        (lane < HEAD_DIM).astype(F32).astype(BF16),
        (lane >= HEAD_DIM).astype(F32).astype(BF16),
    ]
    scaling = HEAD_DIM ** (-0.5)

    def project(source, base, weight, target, rows):
        left = source[pl.ds(base, BLOCK), :]
        for n in range(3):
            target[pl.ds(rows, BLOCK), 256 * n : 256 * n + 256] = dot_nt(
                left, weight[256 * n : 256 * n + 256, :]
            ).astype(BF16)

    def attend(which, qkv, code_row, pairs):
        def pair(k):
            lanes = pl.ds(aligned(k * 128, 128), 128)
            key = qkv[1, :, lanes]
            value_t = jnp.transpose(qkv[2, :, lanes])

            def block(i, rows):
                query = qkv[0, pl.ds(rows, BLOCK), lanes] * jnp.asarray(scaling, BF16)
                query_code = codes[
                    pl.ds(code_row, 1), pl.ds(aligned(own_base + rows, BLOCK), BLOCK)
                ]
                allowed = kcode[which, :, 0:1] == query_code
                for h in range(2):
                    scores = dot_nt(key, query * head_lanes[h])
                    scores = jnp.where(allowed, scores, -1e30)
                    top = jnp.max(scores, axis=0, keepdims=True)
                    exponent = jnp.exp(scores - top)
                    total = jnp.sum(exponent, axis=0, keepdims=True)
                    probs = (exponent * (1.0 / total)).astype(BF16)
                    lse[which, pl.ds(2 * k + h, 1), pl.ds(rows, BLOCK)] = top + jnp.log(total)
                    ctx_t[
                        which,
                        pl.ds(aligned(k * 128 + h * 64, 64), 64),
                        pl.ds(rows, BLOCK),
                    ] = dot_nn(value_t[64 * h : 64 * h + 64, :], probs).astype(BF16)

            blocks(block)

        def run(k, carry):
            pair(k)
            return carry

        lax.fori_loop(pairs[0], pairs[1], run, 0)

    def normalize(summed, index, slot, rows):
        center = summed - jnp.mean(summed, axis=-1, keepdims=True)
        inverse = lax.rsqrt(jnp.mean(center * center, axis=-1, keepdims=True) + NORM_EPSILON)
        normed = center * inverse
        xh[slot, pl.ds(rows, BLOCK), :] = normed.astype(BF16)
        rstd[slot, pl.ds(rows, BLOCK), :] = inverse
        return normed * gains[pl.ds(index, 1), :] + biases[pl.ds(index, 1), :]

    def attention_out(which, rows):
        context = jnp.transpose(ctx_t[which, :, pl.ds(rows, BLOCK)])
        return dot_nn(context, wa[which, 3])

    for copy in own_copies[:1]:
        copy.wait()
    advance(position[(CROSS, 3)])
    for m in range(1, 4):
        last(m)
    blocks(lambda i, rows: project(xrow, own_base + rows, wa.at[CROSS, 0], qkv1.at[0], rows))
    for k in range(1, 3):
        project(xrow, other_base, wa.at[CROSS, k], qkv1.at[k], 0)
        project(xrow, 512, wa.at[CROSS, k], qkv1.at[k], BLOCK)
    attend(0, qkv1, 0, (0, 3))
    advance(position[(SELF, 1)])
    attend(0, qkv1, 0, (3, 6))
    advance(position[(SELF, 2)])

    def cross_end(i, rows):
        stream = xrow[pl.ds(aligned(own_base + rows, BLOCK), BLOCK), :].astype(F32)
        section = normalize(stream + attention_out(0, rows), 0, 0, rows)
        res[pl.ds(rows, BLOCK), :] = section
        sb[pl.ds(rows, BLOCK), :] = section.astype(BF16)

    blocks(cross_end)

    own_copies[1].wait()
    advance(position[(SELF, 3)])
    for k in range(3):
        blocks(lambda i, rows: project(sb, rows, wa.at[SELF, k], qkv2.at[k], rows))
    attend(1, qkv2, 2, (0, 3))
    advance(position[(UP, 1)])
    attend(1, qkv2, 2, (3, 6))
    advance(position[(UP, 2)])

    def self_end(i, rows):
        summed = res[pl.ds(rows, BLOCK), :] + attention_out(1, rows)
        section = normalize(summed, 1 + c, 1, rows)
        res[pl.ds(rows, BLOCK), :] = section
        s2all[0, pl.ds(rows, BLOCK), :] = section.astype(BF16)

    blocks(self_end)

    late = []

    def plane_gather(buffer):
        to_x, to_y, from_x, from_y = new_id(), new_id(), new_id(), new_id()

        def sized(action):
            for core in range(2):

                @pl.when(c == core)
                def _():
                    action(BLOCK * (core + 1))

        def part(k, low, size):
            return buffer.at[k, pl.ds(low, size), :]

        def firsts(size):
            return [
                remote(part(0, 0, size), part(1, 0, size), at(d_x, t), to_x),
                remote(part(0, 0, size), part(2, 0, size), at(d_y, t), to_y),
            ]

        def seconds(size):
            half = size // 2
            return [
                remote(part(1, 0, half), part(3, 0, half), at(d_y, t), from_x),
                remote(part(2, half, half), part(3, half, half), at(d_x, t), from_y),
            ]

        def begin():
            sized(lambda size: [copy.start() for copy in firsts(size)])

        def relay():
            def action(size):
                onward = seconds(size)
                arrive(part(1, 0, size), to_x)
                onward[0].start()
                arrive(part(2, 0, size), to_y)
                onward[1].start()

            sized(action)

        def finish():
            def action(size):
                half = size // 2
                arrive(part(3, 0, half), from_x)
                arrive(part(3, half, half), from_y)

            sized(action)

        def close():
            sized(lambda size: [copy.wait_send() for copy in firsts(size) + seconds(size)])

        late.append(close)
        return begin, relay, finish

    s2_begin, s2_relay, s2_finish = plane_gather(s2all)
    z3_begin, z3_relay, z3_finish = plane_gather(zall)
    def feed_up(shard):
        def block(i, rows):
            left = s2all[0, pl.ds(rows, BLOCK), :]
            for n in range(3):
                cols = slice(256 * n, 256 * n + 256)
                upward = dot_nt(left, wf[0, shard, cols, :])
                cumulative = 0.5 * (1.0 + lax.erf(upward * (0.5**0.5)))
                density = jnp.exp(-0.5 * upward * upward) * 0.3989422804014327
                act[shard, pl.ds(rows, BLOCK), cols] = (upward * cumulative).astype(BF16)
                gp[shard, pl.ds(rows, BLOCK), cols] = (cumulative + upward * density).astype(BF16)

        blocks(block)

    feed_up(t)
    for m in range(1, 4):
        advance(position[(UP, m)])
        feed_up(arrivals[m])

    def feed_down(shard):
        def block(i, rows):
            left = act[shard, pl.ds(rows, BLOCK), :]
            for n in range(3):
                cols = slice(256 * n, 256 * n + 256)
                res[pl.ds(rows, BLOCK), cols] += dot_nn(left, wf[1, shard, :, cols])

        blocks(block)

    own_copies[2].wait()
    feed_down(t)
    for m in range(1, 4):
        advance(position[(DOWN, m)])
        if m == 3:
            s2_begin()
            og_relay()
        feed_down(arrivals[m])

    def layer_end(i, rows):
        result = normalize(res[pl.ds(rows, BLOCK), :], 3 + c, 2, rows)
        yb[pl.ds(rows, BLOCK), :] = result.astype(BF16)

    blocks(layer_end)

    def return_row(target):
        idents = [[new_id() for _ in range(3)] for _ in range(2)]
        send_base = new_id(12)
        local_ids = [local_counter[0] + k for k in range(3)]
        local_counter[0] += 3

        def each(action):
            for k in range(12):
                source_core = 0 if k < 4 else 1
                slots, part = k // 3, k % 3
                src = yb.at[pl.ds(64 * k - 256 * source_core, 64), :]
                for r in range(2):
                    dst = target.at[r, pl.ds(64 * part, 64), :]
                    mine = jnp.logical_and(c == source_core, turn == r)
                    here = jnp.logical_and(holder == c, t == slots)

                    @pl.when(jnp.logical_and(mine, here))
                    def _():
                        copy = pltpu.make_async_copy(src, dst, local_sems.at[local_ids[part]])
                        if action == "start":
                            copy.start()
                        elif action == "wait":
                            copy.wait()

                    @pl.when(jnp.logical_and(mine, jnp.logical_not(here)))
                    def _():
                        copy = remote(
                            src, dst, at(d_holder, slots), send_base + k, idents[r][part]
                        )
                        if action == "start":
                            copy.start()
                        elif action == "wait":
                            copy.wait_send()

        def begin():
            each("start")

        def close():
            each("wait")
            for r in range(2):
                for part in range(3):
                    dst = target.at[r, pl.ds(64 * part, 64), :]
                    k = 3 * t + part
                    source_core = jnp.where(k < 4, 0, 1)
                    from_here = jnp.logical_and(
                        jnp.logical_and(source_core == c, turn == r), holder == c
                    )

                    @pl.when(jnp.logical_not(from_here))
                    def _():
                        arrive(dst, idents[r][part])

        return begin, close

    y_begin, y_close = return_row(y_out)
    y_begin()
    og_finish()

    def grad_view(g, unit, shard, half, low, count):
        rows = pl.ds(aligned(192 * shard + unit * low, 16), unit * count)
        if g == SELF:
            return wa.at[SELF, pl.ds(2 * half, 2), rows, :]
        return wa.at[CROSS, 2 * c + half, rows, :]

    def out_view(g, unit, half, low):
        rows = pl.ds(aligned(unit * low, 16), unit)
        if g == SELF:
            return self_out.at[c, pl.ds(2 * half, 2), rows, :]
        return cross_out.at[2 * c + half, rows, :]

    def out_whole(g, owner):
        if g == SELF:
            return self_out.at[owner]
        return cross_out.at[pl.ds(2 * owner, 2)]

    buffers = {
        "self": (
            lambda half, shard: gp.at[pl.ds(2 * half, 2), pl.ds(96 * shard, 96), :],
            lambda half, shard: r2s.at[half, shard],
            lambda half, m: r3s.at[m - 1, half],
        ),
        "cross": (
            lambda half, shard: ogrow.at[pl.ds(384 * half + 96 * shard, 96), :],
            lambda half, shard: r2c.at[half, shard],
            lambda half, m: r3c.at[m - 1, half],
        ),
    }

    own_quarter = [2 * px + py, px + 2 * py]
    own_pair = [2 * px, 2 * py]
    far_pair = [2 * (1 - px), 2 * (1 - py)]
    far_quarter = [2 * px + (1 - py), (1 - px) + 2 * py]
    near_quarter = {
        "x": [2 * (1 - px) + py, (1 - px) + 2 * py],
        "y": [2 * px + (1 - py), px + 2 * (1 - py)],
    }
    opposite = [2 * (1 - px) + (1 - py), (1 - px) + 2 * (1 - py)]
    first_way = [d_x, d_y]
    second_way = [d_y, d_x]

    def fold(target, pieces):
        shape = target.shape
        if len(shape) == 3:
            for a in range(shape[0]):
                fold(target.at[a], [piece.at[a] for piece in pieces])
            return
        for low in range(0, shape[0], 96):
            rows = slice(low, min(low + 96, shape[0]))
            total = target[rows, :].astype(F32)
            for piece in pieces:
                total = total + piece[rows, :].astype(F32)
            target[rows, :] = total.astype(BF16)

    class Sum:
        def __init__(self, name, g, unit):
            self.g, self.unit = g, unit
            self.first, self.second, self.third = buffers[name]
            self.shards = [0, 1, 2, 3]
            self.s1 = [new_id(4) for _ in range(2)]
            self.s2 = [new_id(4) for _ in range(2)]
            self.s3 = [new_id(4) for _ in range(2)]
            self.to_x = [new_id() for _ in range(2)]
            self.to_y = [new_id() for _ in range(2)]
            self.across = [new_id() for _ in range(2)]
            self.core = new_id()
            self.keep = local_counter[0]
            local_counter[0] += 2
            self.copies = []

        def grad(self, shard, half, low, count):
            return grad_view(self.g, self.unit, shard, half, low, count)

        def out(self, half, low):
            return out_view(self.g, self.unit, half, low)

        def start(self, half, k):
            send(
                self.grad(self.shards[k], half, far_pair[half], 2),
                self.first(half, k),
                at(first_way[half], t),
                self.s1[half] + k,
            )

        def start_all(self):
            for k in range(len(self.shards)):
                for half in range(2):
                    self.start(half, k)

        def stage2(self, half):
            for k, shard in enumerate(self.shards):
                buffer = self.first(half, k)
                arrive(buffer, self.s1[half] + k)
                fold(self.grad(shard, half, far_quarter[half], 1), [self.part(buffer, half, 1)])
                send(
                    self.grad(shard, half, far_quarter[half], 1),
                    self.second(half, k),
                    at(second_way[half], t),
                    self.s2[half] + k,
                )
            for k, shard in enumerate(self.shards):
                buffer = self.first(half, k)
                fold(self.grad(shard, half, own_quarter[half], 1), [self.part(buffer, half, 0)])

        def part(self, buffer, half, other):
            inner = py if half == 0 else px
            low = aligned(self.unit * ((1 - inner) if other else inner), 16)
            rows = pl.ds(low, self.unit)
            if self.g == SELF:
                return buffer.at[:, rows, :]
            return buffer.at[rows, :]

        def stage3(self, half):
            for k, shard in enumerate(self.shards):
                buffer = self.second(half, k)
                arrive(buffer, self.s2[half] + k)
                fold(self.grad(shard, half, own_quarter[half], 1), [buffer])
            for m in range(1, 4):
                send(
                    self.grad((t + m) % 4, half, own_quarter[half], 1),
                    self.third(half, m),
                    at(d, (t + m) % 4),
                    self.s3[half] + m,
                )

        def stage4(self, half):
            pieces = []
            for m in range(1, 4):
                buffer = self.third(half, m)
                arrive(buffer, self.s3[half] + m)
                pieces.append(buffer)
            fold(self.grad(t, half, own_quarter[half], 1), pieces)
            self.publish(half)

        def publish(self, half):
            total = self.grad(t, half, own_quarter[half], 1)
            spot = self.out(half, own_quarter[half])
            copy = pltpu.make_async_copy(total, spot, local_sems.at[self.keep + half])
            copy.start()
            self.copies.append(copy)
            send(total, spot, at(d_x, t), self.to_x[half])
            send(total, spot, at(d_y, t), self.to_y[half])

        def stage5(self):
            for half, way, ids in ((0, "x", self.to_x), (1, "y", self.to_y)):
                for other in range(2):
                    arrive(self.out(other, near_quarter[way][other]), ids[other])
                piece = self.out(half, near_quarter[way][half])
                send(piece, piece, at(d_y if way == "x" else d_x, t), self.across[half])

        def stage6(self):
            for half in range(2):
                arrive(self.out(half, opposite[half]), self.across[half])
            for copy in self.copies:
                copy.wait()
            mine = out_whole(self.g, c)
            send(mine, mine, at(d_core, t), self.core)

        def stage7(self):
            arrive(out_whole(self.g, 1 - c), self.core)

        def both(self, stage):
            return [functools.partial(stage, 0), functools.partial(stage, 1)]

    sum_self = Sum("self", SELF, 48)
    sum_cross = Sum("cross", CROSS, 48)

    class Quarter:
        def __init__(self, k, target):
            self.k, self.target = k, target
            self.base = new_id(4)
            self.to_x, self.to_y = new_id(), new_id()
            self.from_x, self.from_y = new_id(), new_id()
            self.core = new_id()
            self.keep = local_counter[0]
            local_counter[0] += 1

        def rows(self, quarter, low=0, size=192):
            return pl.ds(aligned(192 * quarter + low, 16), size)

        def start(self, m):
            shard = (t + m) % 4
            send(
                wf.at[self.k, shard, self.rows(q), :],
                rq.at[self.k, m - 1],
                at(d, shard),
                self.base + m,
            )

        def collect(self):
            for m in range(1, 4):
                arrive(rq.at[self.k, m - 1], self.base + m)
            total = wf.at[self.k, t, self.rows(q), :]
            fold(total, [rq.at[self.k, m] for m in range(3)])
            spot = self.target.at[c, self.rows(q), :]
            self.copy = pltpu.make_async_copy(total, spot, local_sems.at[self.keep])
            self.copy.start()
            send(total, spot, at(d_x, t), self.to_x)
            send(total, spot, at(d_y, t), self.to_y)

        def relay(self):
            arrive(self.target.at[c, self.rows(qx), :], self.to_x)
            part = self.target.at[c, self.rows(qx, 0, 96), :]
            send(part, part, at(d_y, t), self.from_x)
            arrive(self.target.at[c, self.rows(qy), :], self.to_y)
            part = self.target.at[c, self.rows(qy, 96, 96), :]
            send(part, part, at(d_x, t), self.from_y)

        def swap(self):
            arrive(self.target.at[c, self.rows(qd, 0, 96), :], self.from_x)
            arrive(self.target.at[c, self.rows(qd, 96, 96), :], self.from_y)
            self.copy.wait()
            send(self.target.at[c], self.target.at[c], at(d_core, t), self.core)

        def end(self):
            arrive(self.target.at[1 - c], self.core)

    quarters = [Quarter(0, up_out), Quarter(1, down_out)]

    def quarter_grads(m):
        shard = (t + m) % 4
        own_rows = pl.ds(aligned(192 * q, 16), 192)
        qacc[...] = jnp.zeros_like(qacc)

        def row(r):
            def block(i, rows):
                section = s2all[r, pl.ds(rows, BLOCK), :]
                grad = zall[r, pl.ds(rows, BLOCK), :]
                upward = dot_nt(wf[0, shard, own_rows, :], section)
                cumulative = 0.5 * (1.0 + lax.erf(upward * (0.5**0.5)))
                density = jnp.exp(-0.5 * upward * upward) * 0.3989422804014327
                active = (upward * cumulative).astype(BF16)
                slope = cumulative + upward * density
                up_grad = (dot_nt(wf[1, shard, own_rows, :], grad) * slope).astype(BF16)
                for n in range(3):
                    cols = slice(256 * n, 256 * n + 256)
                    qacc[0, :, cols] += dot_nn(up_grad, section[:, cols])
                    qacc[1, :, cols] += dot_nn(active, grad[:, cols])

            blocks(block)

        times(4, row)
        for k in range(2):
            wf[k, shard, own_rows, :] = qacc[k].astype(BF16)
            if m:
                quarters[k].start(m)

    def norm_back(upstream, index, slot, rows, target):
        normed = xh[slot, pl.ds(rows, BLOCK), :].astype(F32)
        nrm[pl.ds(index, 1), :] += jnp.sum(upstream * normed, axis=0, keepdims=True)
        nrm[pl.ds(index + 8, 1), :] += jnp.sum(upstream, axis=0, keepdims=True)
        scaled = upstream * gains[pl.ds(index, 1), :]
        grad = rstd[slot, pl.ds(rows, BLOCK), :] * (
            scaled
            - jnp.mean(scaled, axis=-1, keepdims=True)
            - normed * jnp.mean(scaled * normed, axis=-1, keepdims=True)
        )
        res[pl.ds(rows, BLOCK), :] = grad
        target[pl.ds(rows, BLOCK), :] = grad.astype(BF16)

    def out_back(i, rows):
        upstream = ogrow[pl.ds(aligned(own_base + rows, BLOCK), BLOCK), :].astype(F32)
        norm_back(upstream, 3 + c, 2, rows, zall.at[0])

    blocks(out_back)
    z3_begin()
    og_close()
    for device in (d_x, d_y):
        pl.semaphore_signal(credit.at[0], inc=1, device_id=at(device, t), device_id_type=MESH)

    def down_back(shard):
        def block(i, rows):
            left = zall[0, pl.ds(rows, BLOCK), :]
            for n in range(3):
                cols = slice(256 * n, 256 * n + 256)
                active_grad = dot_nt(left, wf[1, shard, cols, :])
                slope = gp[shard, pl.ds(rows, BLOCK), cols].astype(F32)
                gp[shard, pl.ds(rows, BLOCK), cols] = (active_grad * slope).astype(BF16)

        blocks(block)

    times(4, down_back)
    s2_relay()

    def up_input(i, rows):
        for n in range(3):
            cols = slice(256 * n, 256 * n + 256)
            total = res[pl.ds(rows, BLOCK), cols]
            for shard in range(4):
                total = total + dot_nn(gp[shard, pl.ds(rows, BLOCK), :], wf[0, shard, :, cols])
            acc[pl.ds(rows, BLOCK), cols] = total

    blocks(up_input)
    z3_relay()
    for device in (d_x, d_y):
        pl.semaphore_signal(credit.at[1], inc=1, device_id=at(device, t), device_id_type=MESH)

    blocks(lambda i, rows: norm_back(acc[pl.ds(rows, BLOCK), :], 1 + c, 1, rows, dzb))

    dctx = act.at[0]

    def context_back(which):
        def block(i, rows):
            left = dzb[pl.ds(rows, BLOCK), :]
            for n in range(3):
                cols = slice(256 * n, 256 * n + 256)
                dctx[pl.ds(rows, BLOCK), cols] = dot_nt(left, wa[which, 3, cols, :]).astype(BF16)

        blocks(block)

    def weight_rows(which, member, left_ref, rights):
        def tile(n):
            rows = aligned(n * 256, 256)
            for k in range(3):
                wide = slice(256 * k, 256 * k + 256)
                total = None
                for low, size, ref in rights:
                    term = dot_nn(
                        left_ref[pl.ds(rows, 256), low : low + size], ref[:, wide]
                    )
                    total = term if total is None else total + term
                wa[which, member, pl.ds(rows, 256), wide] = total.astype(BF16)

        times(3, tile)

    def attend_back(which, qkv, code_row, pairs):
        def pair(k, carry):
            lanes = pl.ds(aligned(k * 128, 128), 128)
            key = qkv[1, :, lanes]
            value = qkv[2, :, lanes]
            key_t = jnp.transpose(key)
            kv_acc[...] = jnp.zeros_like(kv_acc)

            def block(i, rows):
                query = qkv[0, pl.ds(rows, BLOCK), lanes] * jnp.asarray(scaling, BF16)
                grad = dctx[pl.ds(rows, BLOCK), lanes]
                query_code = codes[
                    pl.ds(code_row, 1), pl.ds(aligned(own_base + rows, BLOCK), BLOCK)
                ]
                allowed = kcode[which, :, 0:1] == query_code
                for h in range(2):
                    query_h = query * head_lanes[h]
                    grad_h = grad * head_lanes[h]
                    scores = jnp.where(allowed, dot_nt(key, query_h), -1e30)
                    probs = jnp.exp(
                        scores - lse[which, pl.ds(2 * k + h, 1), pl.ds(rows, BLOCK)]
                    )
                    probs_grad = dot_nt(value, grad_h)
                    delta = jnp.sum(probs * probs_grad, axis=0, keepdims=True)
                    score_grad = (probs * (probs_grad - delta)).astype(BF16)
                    kv_acc[0] += dot_nn(score_grad, query_h)
                    kv_acc[1] += dot_nn(probs.astype(BF16), grad_h)
                    tt[
                        0, pl.ds(aligned(k * 128 + h * 64, 64), 64), pl.ds(rows, BLOCK)
                    ] = (dot_nn(key_t[64 * h : 64 * h + 64, :], score_grad) * scaling).astype(BF16)

            blocks(block)
            for m in range(2):
                tt[1 + m, pl.ds(aligned(k * 128, 128), 128), :] = jnp.transpose(
                    kv_acc[m]
                ).astype(BF16)
            return carry

        lax.fori_loop(pairs[0], pairs[1], pair, 0)

    def pump(*steps):
        for step in steps:
            step()

    context_back(SELF)
    for wait in pending:
        wait()
    pending.clear()
    weight_rows(SELF, 3, ctx_t.at[1], [(0, 512, dzb)])
    attend_back(1, qkv2, 2, (0, 6))

    def self_input(i, rows):
        parts = [jnp.transpose(tt[m, :, pl.ds(rows, BLOCK)]) for m in range(3)]
        for n in range(3):
            cols = slice(256 * n, 256 * n + 256)
            total = res[pl.ds(rows, BLOCK), cols]
            for m in range(3):
                total = total + dot_nn(parts[m], wa[SELF, m, :, cols])
            acc[pl.ds(rows, BLOCK), cols] = total

    blocks(self_input)
    for m in range(3):
        weight_rows(SELF, m, tt.at[m], [(0, 512, sb)])
    pl.semaphore_wait(credit.at[1], 2)
    sum_self.start_all()
    pl.semaphore_signal(credit.at[2], inc=1, device_id=at(d_core, t), device_id_type=MESH)

    s2_finish()
    z3_finish()
    quarter_grads(1)
    quarter_grads(2)
    pump(*sum_self.both(sum_self.stage2))
    quarter_grads(3)
    quarter_grads(0)
    pump(*sum_self.both(sum_self.stage3))

    blocks(lambda i, rows: norm_back(acc[pl.ds(rows, BLOCK), :], 0, 0, rows, dzb))

    norm_ids = [new_id() for _ in range(5)]
    norm_ways = [
        at(d_core, t),
        at(d_x, t),
        at(d_y, t),
        at(d, t + 1 - 2 * (t % 2)),
        at(d, (t + 2) % 4),
    ]
    norm_steps = []

    def norm_begin(k):
        send(nrm if k == 0 else nrm_recv.at[k - 1, 1], nrm_recv.at[k, 0], norm_ways[k], norm_ids[k])

    def norm_step(k):
        arrive(nrm_recv.at[k, 0], norm_ids[k])
        mine = nrm[...] if k == 0 else nrm_recv[k - 1, 1]
        total = mine + nrm_recv[k, 0]
        if k < 4:
            nrm_recv[k, 1] = total
            norm_begin(k + 1)
        else:
            norm_out[...] = total

    norm_begin(0)
    context_back(CROSS)
    weight_rows(CROSS, 3, ctx_t.at[0], [(0, 512, dzb)])
    norm_step(0)
    attend_back(0, qkv1, 0, (0, 3))
    norm_step(1)
    pump(*[one.collect for one in quarters])
    attend_back(0, qkv1, 0, (3, 6))
    norm_step(2)
    pump(*sum_self.both(sum_self.stage4), *[one.relay for one in quarters])

    key_ids = [new_id() for _ in range(2)]

    def key_input(j):
        parts = [jnp.transpose(tt[m, :, 256 * j : 256 * j + 256]) for m in (1, 2)]
        for n in range(3):
            cols = slice(256 * n, 256 * n + 256)
            act[1, 256 * j : 256 * j + 256, cols] = (
                dot_nn(parts[0], wa[CROSS, 1, :, cols]) + dot_nn(parts[1], wa[CROSS, 2, :, cols])
            ).astype(BF16)

    key_input(0)
    key_input(1)
    key_copies = [
        remote(
            act.at[1, pl.ds(256 * j, 256), :],
            dhk_recv.at[j],
            at(d_core, t),
            key_ids[j],
        )
        for j in range(2)
    ]
    key_copies[0].start()

    @pl.when(c == 0)
    def _():
        key_copies[1].start()

    def cross_input(i, rows):
        part = jnp.transpose(tt[0, :, pl.ds(rows, BLOCK)])
        for n in range(3):
            cols = slice(256 * n, 256 * n + 256)
            res[pl.ds(rows, BLOCK), cols] += dot_nn(part, wa[CROSS, 0, :, cols])

    blocks(cross_input)
    weight_rows(CROSS, 0, tt.at[0], [(0, 512, xrow.at[pl.ds(own_base, 512), :])])
    for m in range(1, 3):
        weight_rows(
            CROSS,
            m,
            tt.at[m],
            [
                (0, 256, xrow.at[pl.ds(other_base, 256), :]),
                (256, 256, xrow.at[pl.ds(512, 256), :]),
            ],
        )

    pl.semaphore_wait(credit.at[2], 1)
    core_sums = [(a, n, new_id()) for a in range(2) for n in range(3)]

    def core_slot(a, n):
        k = 3 * a + n
        return qkv2.at[k // 2, pl.ds(256 * (k % 2), 256), :]

    for a, n, ident in core_sums:
        send(
            wa.at[CROSS, 2 * (1 - c) + a, pl.ds(256 * n, 256), :],
            core_slot(a, n),
            at(d_core, t),
            ident,
        )
    norm_step(3)

    y_close()
    arrive(dhk_recv.at[0], key_ids[0])

    @pl.when(c == 1)
    def _():
        arrive(dhk_recv.at[1], key_ids[1])

    yb[:BLOCK, :] = (res[:BLOCK, :] + dhk_recv[0].astype(F32)).astype(BF16)

    @pl.when(c == 1)
    def _():
        own_part = act[1, BLOCK:, :].astype(F32)
        yb[BLOCK:, :] = (res[BLOCK:, :] + dhk_recv[1].astype(F32) + own_part).astype(BF16)

    dx_begin, dx_close = return_row(dx_out)
    dx_begin()

    for a, n, ident in core_sums:
        arrive(core_slot(a, n), ident)
        fold(wa.at[CROSS, 2 * c + a, pl.ds(256 * n, 256), :], [core_slot(a, n)])
    pl.semaphore_wait(credit.at[0], 2)
    sum_cross.start_all()
    norm_step(4)
    pump(
        *[one.swap for one in quarters],
        sum_self.stage5,
        *sum_cross.both(sum_cross.stage2),
        sum_self.stage6,
        *sum_cross.both(sum_cross.stage3),
        *sum_cross.both(sum_cross.stage4),
        sum_cross.stage5,
        sum_cross.stage6,
        *[one.end for one in quarters],
        sum_self.stage7,
        sum_cross.stage7,
    )
    for wait in pending + late:
        wait()
    key_copies[0].wait_send()

    @pl.when(c == 0)
    def _():
        key_copies[1].wait_send()

    dx_close()
    if counter[0] > SEMAPHORES or local_counter[0] > LOCALS:
        raise ValueError((counter[0], local_counter[0]))


SEMAPHORES = 320
LOCALS = 40


def call_layer(*operands):
    def vmem(shape, dtype=BF16):
        return pltpu.VMEM(shape, dtype)

    anywhere = pl.BlockSpec(memory_space=pl.ANY)
    whole = pl.BlockSpec(memory_space=pltpu.VMEM)
    x_in = operands[0]
    return pl.pallas_call(
        layer_kernel,
        name="cross_modality_layer",
        out_shape=(
            jax.ShapeDtypeStruct(x_in.shape, BF16),
            jax.ShapeDtypeStruct(x_in.shape, BF16),
            jax.ShapeDtypeStruct((4, 192, 768), BF16),
            jax.ShapeDtypeStruct((2, 4, 192, 768), BF16),
            jax.ShapeDtypeStruct((2, 768, 768), BF16),
            jax.ShapeDtypeStruct((2, 768, 768), BF16),
            jax.ShapeDtypeStruct((16, 768), F32),
        ),
        in_specs=[anywhere] * 7 + [whole] * 2,
        out_specs=(anywhere,) * 6 + (whole,),
        scratch_shapes=[
            vmem((2, 4, 768, 768)),
            vmem((2, 4, 768, 768)),
            vmem((768, 768)),
            vmem((768, 768)),
            vmem((8, 768), F32),
            vmem((2, 512, 128), F32),
            vmem((3, 512, 768)),
            vmem((3, 512, 768)),
            vmem((2, 768, 512)),
            vmem((2, 16, 512), F32),
            vmem((3, 512, 768)),
            vmem((3, 512, 1), F32),
            vmem((512, 768)),
            vmem((512, 768), F32),
            vmem((512, 768), F32),
            vmem((4, 512, 768)),
            vmem((4, 512, 768)),
            vmem((512, 768)),
            vmem((3, 768, 512)),
            vmem((512, 768)),
            vmem((2, 256, 768)),
            vmem((2, 512, 128), F32),
            vmem((16, 768), F32),
            vmem((5, 2, 16, 768), F32),
            vmem((4, 512, 768)),
            vmem((4, 512, 768)),
            vmem((2, 192, 768), F32),
            vmem((2, 3, 192, 768)),
            vmem((2, 4, 2, 48, 768)),
            vmem((3, 2, 2, 48, 768)),
            vmem((2, 4, 48, 768)),
            vmem((3, 2, 48, 768)),
            pltpu.SemaphoreType.DMA((SEMAPHORES,)),
            pltpu.SemaphoreType.DMA((SEMAPHORES,)),
            pltpu.SemaphoreType.DMA((LOCALS,)),
            pltpu.SemaphoreType.REGULAR((3,)),
        ],
        compiler_params=pltpu.CompilerParams(
            collective_id=0, has_side_effects=True, vmem_limit_bytes=64 * 1024 * 1024 - 512 * 1024
        ),
    )(*operands)


def solution(mesh):
    extra = []
    step = 8
    while step < mesh.shape["dp"]:
        extra.append(step)
        step *= 2

    def total(array):
        for step in extra:
            pairs = [(k, k ^ step) for k in range(mesh.shape["dp"])]
            array = array + lax.ppermute(array, "dp", pairs)
        return array

    def body(
        layer_input,
        word_segments,
        image_order,
        cross_qkv,
        cross_out,
        self_qkv,
        self_out,
        ffn_up,
        ffn_down,
        norm_gains,
        norm_biases,
        out_grad,
    ):
        rows = layer_input.shape[0]
        images = jnp.repeat(image_order, BOXES, axis=1)
        pads = jnp.full((rows, PADS), CAPTIONS, jnp.int32)
        none = jnp.full((rows, WORDS + REGIONS + PADS), -1, jnp.int32)
        groups = jnp.concatenate([word_segments, images, pads], axis=1)
        keys = jnp.concatenate([word_segments, none[:, :REGIONS], pads], axis=1)
        kinds = jnp.concatenate([word_segments, images + 16, pads + 32], axis=1)
        codes = jnp.stack([groups, keys, kinds, none, none, none, none, none], axis=1).astype(F32)
        cross = jnp.concatenate([jnp.swapaxes(cross_qkv, 1, 2), cross_out[None]], axis=0)
        own = jnp.concatenate([jnp.swapaxes(self_qkv, 2, 3), self_out[:, None]], axis=1)
        y, dx, d_cross, d_self, d_up, d_down, d_norm = call_layer(
            layer_input,
            out_grad,
            codes,
            cross,
            own,
            ffn_up,
            ffn_down,
            norm_gains,
            norm_biases,
        )
        d_cross, d_self, d_up, d_down = [
            total(array.astype(F32)) for array in (d_cross, d_self, d_up, d_down)
        ]
        d_norm = total(d_norm)
        return (
            y,
            dx.astype(F32),
            jnp.swapaxes(d_cross[:3], 1, 2),
            d_cross[3],
            jnp.swapaxes(d_self[:, :3], 2, 3),
            d_self[:, 3],
            jnp.swapaxes(d_up, 1, 2),
            d_down,
            d_norm[0:5],
            d_norm[8:13],
        )

    in_specs = (
        P("dp", "tensor", None),
        P("dp", None),
        P("dp", None),
        P(None, None, "tensor"),
        P("tensor", None),
        P(None, None, None, "tensor"),
        P(None, "tensor", None),
        P(None, None, "tensor"),
        P(None, "tensor", None),
        P(),
        P(),
        P("dp", "tensor", None),
    )
    out_specs = (
        P("dp", "tensor", None),
        P("dp", "tensor", None),
        P(None, None, "tensor"),
        P("tensor", None),
        P(None, None, None, "tensor"),
        P(None, "tensor", None),
        P(None, None, "tensor"),
        P(None, "tensor", None),
        P(),
        P(),
    )
    return jax.shard_map(body, mesh=mesh, in_specs=in_specs, out_specs=out_specs, check_vma=False)
```

profile of v0, /device:TPU:0, one launch (start us, length us, event | category | flops | bytes accessed | tf_op | source)
XLA Modules:
  0.0 326.0 jit_solution(15471438794597196612)
XLA Ops:
  0.6 0.7 broadcast_in_dim.9
  1.4 0.1 reshape.23
  1.5 0.1 pad.12.clone
  1.6 0.1 pad.6.clone
  1.7 0.7 fusion.1
  2.4 0.1 stack.19
  2.5 0.6 convert_element_type.16.codes_in
  3.1 0.0 copy-start.3
  3.1 0.0 copy-start.6
  3.1 3.4 %pad_maximum_fusion.self_in = bf16[2,4,192,768]{3,2,1,0:T(8,128)(2,1)} fusion(bf16[2,1,192,768]{3,2,1,0:T(8,128)(2,1)} %bitcast.16, bf16[2,3,192,768]{3,2,1,0:T(8,128)(2,1)} %bitcast.14), kind=kLoop, calls=%fused_computation.2 | loop fusion | flops 1179648 | bytes 4718592 | tf_op jit(solution)/shard_map/concatenate | solution.py:1334
  6.5 0.0 copy-done.3
  6.5 0.0 copy-done.6
  6.5 1.1 pad_maximum_fusion.1.cross_in
  7.6 296.3 %cross_modality_layer.1 = (bf16[2,192,768]{2,1,0:T(8,128)(2,1)}, bf16[2,192,768]{2,1,0:T(8,128)(2,1)}, bf16[4,192,768]{2,1,0:T(8,128)(2,1)}, bf16[2,4,192,768]{3...) custom-call(bf16[2,192,768]{2,1,0:T(8,128)(2,1)} %x_in.1, ...), custom_call_target="tpu_custom_call" | custom-call | tf_op jit(solution)/shard_map/cross_modality_layer/pallas_call | solution.py:1240
  303.9 2.1 convert_element_type.19
  306.0 2.0 slice_bitcast_fusion
  308.0 0.0 copy-start.2
  308.0 1.1 slice_bitcast_fusion.2
  309.1 0.6 copy-done.2
  309.7 0.2 convert_element_type.18
  309.9 0.0 copy-start.7
  309.9 0.0 copy-start.1
  309.9 1.3 slice_bitcast_fusion.1
  311.3 0.9 slice_bitcast_fusion.3
  312.1 0.0 copy-done.7
  312.1 0.6 fusion.3
  312.7 0.0 copy-done.1
  312.7 2.5 convert_bitcast_fusion
  315.3 0.0 copy-start
  315.3 6.2 %copy.24 = f32[2,768,768]{2,1,0:T(8,128)} copy(f32[2,768,768]{1,2,0:T(8,128)} %convert_bitcast_fusion) | data formatting | bytes 9437184
  321.5 0.0 copy-done
  321.5 0.0 copy-start.4
  321.5 0.0 copy-start.5
  321.5 2.5 convert_element_type.20
  324.0 0.0 copy-done.4
  324.0 1.1 convert_element_type.17
  325.1 0.0 copy-done.5
  325.1 0.8 copy.26
  (10 shorter events, 0.0 us)
Async XLA Ops:
  3.1 3.4 %copy-start.3 = (bf16[3,768,192]{1,2,0:T(8,128)(2,1)S(1)}, bf16[3,768,192]{1,2,0:T(8,128)(2,1)}, u32[]{:S(2)}) copy-start(bf16[3,768,192]{1,2,0:T(8,128)(2,1)} %param.15) | copy-start | bytes 2654212
  3.1 3.4 %copy-start.6 = (bf16[192,768]{1,0:T(8,128)(2,1)S(1)}, bf16[192,768]{1,0:T(8,128)(2,1)}, u32[]{:S(2)}) copy-start(bf16[192,768]{1,0:T(8,128)(2,1)} %param.16) | copy-start | bytes 884740
  308.0 1.7 copy-start.2
  309.9 2.2 copy-start.7
  309.9 2.8 copy-start.1
  315.3 6.2 %copy-start = (bf16[2,768,768]{2,1,0:T(8,128)(2,1)S(1)}, bf16[2,768,768]{2,1,0:T(8,128)(2,1)}, u32[]{:S(2)}) copy-start(bf16[2,768,768]{2,1,0:T(8,128)(2,1)} %get-tuple-element.22) | copy-start | bytes 7077892
  321.5 2.6 copy-start.4
  321.5 3.6 %copy-start.5 = (bf16[2,192,768]{2,1,0:T(8,128)(2,1)S(1)}, bf16[2,192,768]{2,1,0:T(8,128)(2,1)}, u32[]{:S(2)}) copy-start(bf16[2,192,768]{2,1,0:T(8,128)(2,1)} %get-tuple-element.59) | copy-start | bytes 1769476
where the time goes:
time: 326 us
  Pallas kernels  296 us (91%)
  local copies, waits for them, and re-layouts  14.6 us (4%)
  other arithmetic  14.3 us (4%)
    pallas_call x1, Pallas kernels, call_layer(): pl.pallas_call(layer_kernel, name='cross_modality_layer', out_shape=(jax....  296 us
    unnamed x18, local copies, waits for them, and re-layouts  7.64 us

commit v1 on v0

--- a/solution.py
+++ b/solution.py
@@ -38,7 +38,9 @@
     og_in,
     codes_in,
     cross_in,
+    cross_out_in,
     self_in,
+    self_out_in,
     up_in,
     down_in,
     gains,
@@ -160,15 +162,19 @@
 
     half_rows = aligned(t * 192, 16)
     own_copies = [
-        local(cross_in, wa.at[CROSS, :, pl.ds(half_rows, 192), :]),
-        local(self_in.at[c], wa.at[SELF, :, pl.ds(half_rows, 192), :]),
+        local(cross_out_in, wa.at[CROSS, 3, pl.ds(half_rows, 192), :]),
+        local(self_out_in.at[c], wa.at[SELF, 3, pl.ds(half_rows, 192), :]),
         local(down_in.at[c], wf.at[1, t]),
+    ]
+    raw_copies = [
+        local(cross_in, wa.at[CROSS, pl.ds(0, 3), pl.ds(half_rows, 192), :]),
+        local(self_in.at[c], wa.at[SELF, pl.ds(0, 3), pl.ds(half_rows, 192), :]),
     ]
     up_copies = [
         local(up_in.at[c, pl.ds(0, 512), :], qkv1.at[0]),
         local(up_in.at[c, pl.ds(512, 256), :], qkv1.at[1, pl.ds(0, 256), :]),
     ]
-    for copy in own_copies + up_copies:
+    for copy in raw_copies + own_copies + up_copies:
         copy.start()
 
     zero_half = jnp.zeros((BLOCK, 768), BF16)
@@ -182,6 +188,9 @@
         tt[0, :, BLOCK:] = jnp.zeros((768, BLOCK), BF16)
 
     nrm[...] = jnp.zeros_like(nrm)
+    for g in (CROSS, SELF):
+        raw_copies[g].wait()
+        own_copies[g].wait()
     pl.semaphore_wait(barrier, len(partners))
 
     def spread_row(source, row):
@@ -270,10 +279,7 @@
         if g >= UP:
             rows = pl.ds(aligned(q * 192, 16), 192)
             return wf.at[0, t, rows, :] if g == UP else down_in.at[c, rows, :]
-        rows = pl.ds(aligned(q * 48, 16), 48)
-        if g == SELF:
-            return self_in.at[c, :, rows, :]
-        return cross_in.at[pl.ds(2 * c, 2), rows, :]
+        return share(g, t, q, 0, 2)
 
     qx, qy = (1 - px) + 2 * py, px + 2 * (1 - py)
     qd = (1 - px) + 2 * (1 - py)
@@ -481,8 +487,6 @@
         context = jnp.transpose(ctx_t[which, :, pl.ds(rows, BLOCK)])
         return dot_nn(context, wa[which, 3])
 
-    for copy in own_copies[:1]:
-        copy.wait()
     advance(position[(CROSS, 3)])
     for m in range(1, 4):
         last(m)
@@ -503,7 +507,6 @@
 
     blocks(cross_end)
 
-    own_copies[1].wait()
     advance(position[(SELF, 3)])
     for k in range(3):
         blocks(lambda i, rows: project(sb, rows, wa.at[SELF, k], qkv2.at[k], rows))
@@ -717,6 +720,7 @@
     }
     opposite = [2 * (1 - px) + (1 - py), (1 - px) + 2 * (1 - py)]
     first_way = [d_x, d_y]
+    t_pair, t_far, t_cross = t + 1 - 2 * (t % 2), (t + 2) % 4, 3 - t
     second_way = [d_y, d_x]
 
     def fold(target, pieces):
@@ -795,21 +799,31 @@
                 buffer = self.second(half, k)
                 arrive(buffer, self.s2[half] + k)
                 fold(self.grad(shard, half, own_quarter[half], 1), [buffer])
-            for m in range(1, 4):
+            for k, shard in enumerate((t_pair, t_cross)):
                 send(
-                    self.grad((t + m) % 4, half, own_quarter[half], 1),
-                    self.third(half, m),
-                    at(d, (t + m) % 4),
-                    self.s3[half] + m,
+                    self.grad(shard, half, own_quarter[half], 1),
+                    self.third(half, 1 + k),
+                    at(d, t_pair),
+                    self.s3[half] + k,
                 )
 
         def stage4(self, half):
-            pieces = []
-            for m in range(1, 4):
-                buffer = self.third(half, m)
-                arrive(buffer, self.s3[half] + m)
-                pieces.append(buffer)
-            fold(self.grad(t, half, own_quarter[half], 1), pieces)
+            for k, shard in ((1, t_far), (0, t)):
+                buffer = self.third(half, 1 + k)
+                arrive(buffer, self.s3[half] + k)
+                fold(self.grad(shard, half, own_quarter[half], 1), [buffer])
+                if k:
+                    send(
+                        self.grad(t_far, half, own_quarter[half], 1),
+                        self.third(half, 3),
+                        at(d, t_far),
+                        self.s3[half] + 2,
+                    )
+
+        def stage4_end(self, half):
+            buffer = self.third(half, 3)
+            arrive(buffer, self.s3[half] + 2)
+            fold(self.grad(t, half, own_quarter[half], 1), [buffer])
             self.publish(half)
 
         def publish(self, half):
@@ -858,20 +872,23 @@
         def rows(self, quarter, low=0, size=192):
             return pl.ds(aligned(192 * quarter + low, 16), size)
 
-        def start(self, m):
-            shard = (t + m) % 4
-            send(
-                wf.at[self.k, shard, self.rows(q), :],
-                rq.at[self.k, m - 1],
-                at(d, shard),
-                self.base + m,
-            )
+        def piece(self, shard):
+            return wf.at[self.k, shard, self.rows(q), :]
+
+        def start(self):
+            for k, shard in enumerate((t_pair, t_cross)):
+                send(self.piece(shard), rq.at[self.k, k], at(d, t_pair), self.base + k)
+
+        def middle(self):
+            arrive(rq.at[self.k, 1], self.base + 1)
+            fold(self.piece(t_far), [rq.at[self.k, 1]])
+            send(self.piece(t_far), rq.at[self.k, 2], at(d, t_far), self.base + 2)
 
         def collect(self):
-            for m in range(1, 4):
-                arrive(rq.at[self.k, m - 1], self.base + m)
-            total = wf.at[self.k, t, self.rows(q), :]
-            fold(total, [rq.at[self.k, m] for m in range(3)])
+            for k in (0, 2):
+                arrive(rq.at[self.k, k], self.base + k)
+            total = self.piece(t)
+            fold(total, [rq.at[self.k, 0], rq.at[self.k, 2]])
             spot = self.target.at[c, self.rows(q), :]
             self.copy = pltpu.make_async_copy(total, spot, local_sems.at[self.keep])
             self.copy.start()
@@ -897,8 +914,7 @@
 
     quarters = [Quarter(0, up_out), Quarter(1, down_out)]
 
-    def quarter_grads(m):
-        shard = (t + m) % 4
+    def quarter_grads(shard):
         own_rows = pl.ds(aligned(192 * q, 16), 192)
         qacc[...] = jnp.zeros_like(qacc)
 
@@ -922,8 +938,6 @@
         times(4, row)
         for k in range(2):
             wf[k, shard, own_rows, :] = qacc[k].astype(BF16)
-            if m:
-                quarters[k].start(m)
 
     def norm_back(upstream, index, slot, rows, target):
         normed = xh[slot, pl.ds(rows, BLOCK), :].astype(F32)
@@ -960,7 +974,6 @@
         blocks(block)
 
     times(4, down_back)
-    s2_relay()
 
     def up_input(i, rows):
         for n in range(3):
@@ -971,11 +984,11 @@
             acc[pl.ds(rows, BLOCK), cols] = total
 
     blocks(up_input)
-    z3_relay()
     for device in (d_x, d_y):
         pl.semaphore_signal(credit.at[1], inc=1, device_id=at(device, t), device_id_type=MESH)
 
     blocks(lambda i, rows: norm_back(acc[pl.ds(rows, BLOCK), :], 1 + c, 1, rows, dzb))
+    s2_relay()
 
     dctx = act.at[0]
 
@@ -1053,6 +1066,7 @@
     pending.clear()
     weight_rows(SELF, 3, ctx_t.at[1], [(0, 512, dzb)])
     attend_back(1, qkv2, 2, (0, 6))
+    z3_relay()
 
     def self_input(i, rows):
         parts = [jnp.transpose(tt[m, :, pl.ds(rows, BLOCK)]) for m in range(3)]
@@ -1072,12 +1086,10 @@
 
     s2_finish()
     z3_finish()
-    quarter_grads(1)
-    quarter_grads(2)
-    pump(*sum_self.both(sum_self.stage2))
-    quarter_grads(3)
-    quarter_grads(0)
-    pump(*sum_self.both(sum_self.stage3))
+    quarter_grads(t_pair)
+    quarter_grads(t_cross)
+    pump(*[one.start for one in quarters])
+    quarter_grads(t_far)
 
     blocks(lambda i, rows: norm_back(acc[pl.ds(rows, BLOCK), :], 0, 0, rows, dzb))
 
@@ -1110,10 +1122,10 @@
     norm_step(0)
     attend_back(0, qkv1, 0, (0, 3))
     norm_step(1)
-    pump(*[one.collect for one in quarters])
+    pump(*sum_self.both(sum_self.stage2))
     attend_back(0, qkv1, 0, (3, 6))
     norm_step(2)
-    pump(*sum_self.both(sum_self.stage4), *[one.relay for one in quarters])
+    pump(*[one.middle for one in quarters])
 
     key_ids = [new_id() for _ in range(2)]
 
@@ -1161,6 +1173,8 @@
             ],
         )
 
+    pump(*sum_self.both(sum_self.stage3))
+
     pl.semaphore_wait(credit.at[2], 1)
     core_sums = [(a, n, new_id()) for a in range(2) for n in range(3)]
 
@@ -1192,7 +1206,6 @@
         yb[BLOCK:, :] = (res[BLOCK:, :] + dhk_recv[1].astype(F32) + own_part).astype(BF16)
 
     dx_begin, dx_close = return_row(dx_out)
-    dx_begin()
 
     for a, n, ident in core_sums:
         arrive(core_slot(a, n), ident)
@@ -1200,13 +1213,20 @@
     pl.semaphore_wait(credit.at[0], 2)
     sum_cross.start_all()
     norm_step(4)
+    quarter_grads(t)
     pump(
+        *[one.collect for one in quarters],
+        *sum_cross.both(sum_cross.stage2),
+        *sum_self.both(sum_self.stage4),
+        *[one.relay for one in quarters],
+        *sum_cross.both(sum_cross.stage3),
+        dx_begin,
+        *sum_self.both(sum_self.stage4_end),
+        *sum_cross.both(sum_cross.stage4),
         *[one.swap for one in quarters],
         sum_self.stage5,
-        *sum_cross.both(sum_cross.stage2),
+        *sum_cross.both(sum_cross.stage4_end),
         sum_self.stage6,
-        *sum_cross.both(sum_cross.stage3),
-        *sum_cross.both(sum_cross.stage4),
         sum_cross.stage5,
         sum_cross.stage6,
         *[one.end for one in quarters],
@@ -1249,7 +1269,7 @@
             jax.ShapeDtypeStruct((2, 768, 768), BF16),
             jax.ShapeDtypeStruct((16, 768), F32),
         ),
-        in_specs=[anywhere] * 7 + [whole] * 2,
+        in_specs=[anywhere] * 9 + [whole] * 2,
         out_specs=(anywhere,) * 6 + (whole,),
         scratch_shapes=[
             vmem((2, 4, 768, 768)),
@@ -1295,6 +1315,98 @@
     )(*operands)
 
 
+def results_kernel(
+    cross, own, up, down, dx, norm,
+    dx_out, cross_qkv, cross_out, self_qkv, self_out, up_out, down_out, gains, biases,
+    v_cross, v_own, v_up, v_down, v_dx, v_norm,
+    w_dx, w_cross_qkv, w_cross_out, w_self_qkv, w_self_out, w_up, w_down,
+    in_sems, out_sems,
+):
+    sources = [
+        (down.at[0], v_down.at[0]),
+        (down.at[1], v_down.at[1]),
+        (up.at[0], v_up.at[0]),
+        (up.at[1], v_up.at[1]),
+        (own.at[0], v_own.at[0]),
+        (own.at[1], v_own.at[1]),
+        (cross, v_cross),
+        (dx, v_dx),
+        (norm, v_norm),
+    ]
+    loads = [
+        pltpu.make_async_copy(src, dst, in_sems.at[k]) for k, (src, dst) in enumerate(sources)
+    ]
+    for load in loads:
+        load.start()
+    stores = []
+
+    def store(src, dst):
+        copy = pltpu.make_async_copy(src, dst, out_sems.at[len(stores)])
+        copy.start()
+        stores.append(copy)
+
+    for k in range(2):
+        loads[k].wait()
+        w_down[k] = v_down[k].astype(F32)
+        store(w_down.at[k], down_out.at[k])
+    for k in range(2):
+        loads[2 + k].wait()
+        for n in range(3):
+            cols = slice(256 * n, 256 * n + 256)
+            w_up[k, cols, :] = jnp.transpose(v_up[k, :, cols]).astype(F32)
+        store(w_up.at[k], up_out.at[k])
+    for k in range(2):
+        loads[4 + k].wait()
+        for n in range(3):
+            w_self_qkv[k, n] = v_own[k, n].astype(F32)
+        w_self_out[k] = v_own[k, 3].astype(F32)
+        store(w_self_qkv.at[k], self_qkv.at[k])
+        store(w_self_out.at[k], self_out.at[k])
+    loads[6].wait()
+    for n in range(3):
+        w_cross_qkv[n] = v_cross[n].astype(F32)
+    w_cross_out[...] = v_cross[3].astype(F32)
+    store(w_cross_qkv, cross_qkv)
+    store(w_cross_out, cross_out)
+    loads[7].wait()
+    w_dx[...] = v_dx[...].astype(F32)
+    store(w_dx, dx_out)
+    loads[8].wait()
+    gains[...] = v_norm[0:5, :]
+    biases[...] = v_norm[8:13, :]
+    for copy in stores:
+        copy.wait()
+
+
+def call_results(cross, own, up, down, dx, norm):
+    anywhere = pl.BlockSpec(memory_space=pl.ANY)
+    whole = pl.BlockSpec(memory_space=pltpu.VMEM)
+
+    def out(shape):
+        return jax.ShapeDtypeStruct(shape, F32)
+
+    shapes = [
+        dx.shape,
+        (3, 192, 768),
+        (192, 768),
+        (2, 3, 192, 768),
+        (2, 192, 768),
+        (2, 768, 768),
+        (2, 768, 768),
+    ]
+    return pl.pallas_call(
+        results_kernel,
+        name="results",
+        out_shape=tuple(out(shape) for shape in shapes) + (out((5, 768)), out((5, 768))),
+        in_specs=[anywhere] * 6,
+        out_specs=(anywhere,) * 7 + (whole,) * 2,
+        scratch_shapes=[pltpu.VMEM(ref.shape, ref.dtype) for ref in (cross, own, up, down, dx, norm)]
+        + [pltpu.VMEM(shape, F32) for shape in shapes]
+        + [pltpu.SemaphoreType.DMA((9,)), pltpu.SemaphoreType.DMA((11,))],
+        compiler_params=pltpu.CompilerParams(vmem_limit_bytes=56 * 1024 * 1024),
+    )(cross, own, up, down, dx, norm)
+
+
 def solution(mesh):
     extra = []
     step = 8
@@ -1330,35 +1442,24 @@
         keys = jnp.concatenate([word_segments, none[:, :REGIONS], pads], axis=1)
         kinds = jnp.concatenate([word_segments, images + 16, pads + 32], axis=1)
         codes = jnp.stack([groups, keys, kinds, none, none, none, none, none], axis=1).astype(F32)
-        cross = jnp.concatenate([jnp.swapaxes(cross_qkv, 1, 2), cross_out[None]], axis=0)
-        own = jnp.concatenate([jnp.swapaxes(self_qkv, 2, 3), self_out[:, None]], axis=1)
         y, dx, d_cross, d_self, d_up, d_down, d_norm = call_layer(
             layer_input,
             out_grad,
             codes,
-            cross,
-            own,
+            jnp.swapaxes(cross_qkv, 1, 2),
+            cross_out,
+            jnp.swapaxes(self_qkv, 2, 3),
+            self_out,
             ffn_up,
             ffn_down,
             norm_gains,
             norm_biases,
         )
-        d_cross, d_self, d_up, d_down = [
-            total(array.astype(F32)) for array in (d_cross, d_self, d_up, d_down)
-        ]
-        d_norm = total(d_norm)
-        return (
-            y,
-            dx.astype(F32),
-            jnp.swapaxes(d_cross[:3], 1, 2),
-            d_cross[3],
-            jnp.swapaxes(d_self[:, :3], 2, 3),
-            d_self[:, 3],
-            jnp.swapaxes(d_up, 1, 2),
-            d_down,
-            d_norm[0:5],
-            d_norm[8:13],
-        )
+        dx, *grads = call_results(d_cross, d_self, d_up, d_down, dx, d_norm)
+        grads = [total(array) for array in grads]
+        grads[0] = jnp.swapaxes(grads[0], 1, 2)
+        grads[2] = jnp.swapaxes(grads[2], 2, 3)
+        return (y, dx, *grads)
 
     in_specs = (
         P("dp", "tensor", None),

time: 326 us -> 307 us (0.942)
  other arithmetic: 14.3 us -> 1.33 us
  local copies, waits for them, and re-layouts: 14.6 us -> 1.91 us
  Pallas kernels: 296 us -> 302 us
    pallas_call x0 -> x1, Pallas kernels: none -> 9.32 us  [call_results(): pl.pallas_call(results_kernel, name='results', out_shape=tuple((out(shape...]
    unnamed x18 -> x3, local copies, waits for them, and re-layouts: 7.64 us -> 0.82 us
    convert_element_type x4 -> x0, other arithmetic: 5.91 us -> none  [the longest x3 4.82 us: body(): array.astype(F32)]
    concatenate x2 -> x0, other arithmetic: 4.47 us -> none  [the longest x1 3.36 us: body(): jnp.concatenate([jnp.swapaxes(self_qkv, 2, 3), self_out[:, None]], axis=1)]
    transpose x2 -> x0, local copies, waits for them, and re-layouts: 3.34 us -> none  [the longest x1 2.02 us: body(): jnp.swapaxes(d_self[:, :3], 2, 3)]
    pallas_call x1, Pallas kernels: 296 us -> 293 us  [call_layer(): pl.pallas_call(layer_kernel, name='cross_modality_layer', out_shape=(jax....]
where the time goes in v1:
time: 307 us; the launch traced here: 306 us
  Pallas kernels  302 us (98%)
    pallas_call x1, Pallas kernels, call_layer(): pl.pallas_call(layer_kernel, name='cross_modality_layer', out_shape=(jax....  293 us
    pallas_call x1, Pallas kernels, call_results(): pl.pallas_call(results_kernel, name='results', out_shape=tuple((out(shape...  9.32 us

profile of v1, /device:TPU:0, one launch (start us, length us, event | category | flops | bytes accessed | tf_op | source)
XLA Modules:
  0.0 306.2 jit_solution(3367012866161053415)
XLA Ops:
  0.7 0.1 pad.2.clone
  0.8 0.1 pad.8.clone
  0.8 0.7 broadcast_in_dim.3
  1.6 0.1 reshape.23
  1.7 0.7 fusion.1
  2.5 0.1 stack.19
  2.5 0.6 convert_element_type.3.codes_in
  3.1 292.9 %cross_modality_layer.1 = (bf16[2,192,768]{2,1,0:T(8,128)(2,1)}, bf16[2,192,768]{2,1,0:T(8,128)(2,1)}, bf16[4,192,768]{2,1,0:T(8,128)(2,1)}, bf16[2,4,192,768]{3...) custom-call(bf16[2,192,768]{2,1,0:T(8,128)(2,1)} %x_in.1, ...), custom_call_target="tpu_custom_call" | custom-call | tf_op jit(solution)/shard_map/cross_modality_layer/pallas_call | solution.py:1260
  296.1 0.0 copy-start
  296.1 9.3 %results.1 = (f32[2,192,768]{2,1,0:T(8,128)}, f32[3,192,768]{2,1,0:T(8,128)}, f32[192,768]{1,0:T(8,128)}, f32[2,3,192,768]{3,2,1,0:T(8,128)}, f32[2,192,768]{2,1...) custom-call(bf16[4,192,768]{2,1,0:T(8,128)(2,1)} %get-tuple-element.27.cross, ...), custom_call_target="tpu_custom_call" | custom-call | tf_op jit(solution)/shard_map/results/pallas_call | solution.py:1397
  305.4 0.0 copy-done
  305.4 0.8 copy.24
  (10 shorter events, 0.0 us)
Async XLA Ops:
  296.1 9.3 %copy-start = (bf16[2,192,768]{2,1,0:T(8,128)(2,1)S(1)}, bf16[2,192,768]{2,1,0:T(8,128)(2,1)}, u32[]{:S(2)}) copy-start(bf16[2,192,768]{2,1,0:T(8,128)(2,1)} %get-tuple-element.55) | copy-start | bytes 1769476

commit v2 on v1

--- a/solution.py
+++ b/solution.py
@@ -875,20 +875,15 @@
         def piece(self, shard):
             return wf.at[self.k, shard, self.rows(q), :]
 
-        def start(self):
-            for k, shard in enumerate((t_pair, t_cross)):
-                send(self.piece(shard), rq.at[self.k, k], at(d, t_pair), self.base + k)
-
-        def middle(self):
-            arrive(rq.at[self.k, 1], self.base + 1)
-            fold(self.piece(t_far), [rq.at[self.k, 1]])
-            send(self.piece(t_far), rq.at[self.k, 2], at(d, t_far), self.base + 2)
+        def start(self, m):
+            shard = (t + m) % 4
+            send(self.piece(shard), rq.at[self.k, m - 1], at(d, shard), self.base + m)
 
         def collect(self):
-            for k in (0, 2):
-                arrive(rq.at[self.k, k], self.base + k)
+            for m in range(1, 4):
+                arrive(rq.at[self.k, m - 1], self.base + m)
             total = self.piece(t)
-            fold(total, [rq.at[self.k, 0], rq.at[self.k, 2]])
+            fold(total, [rq.at[self.k, m] for m in range(3)])
             spot = self.target.at[c, self.rows(q), :]
             self.copy = pltpu.make_async_copy(total, spot, local_sems.at[self.keep])
             self.copy.start()
@@ -1086,10 +1081,10 @@
 
     s2_finish()
     z3_finish()
-    quarter_grads(t_pair)
-    quarter_grads(t_cross)
-    pump(*[one.start for one in quarters])
-    quarter_grads(t_far)
+    for m in (2, 1, 3):
+        quarter_grads((t + m) % 4)
+        for one in quarters:
+            one.start(m)
 
     blocks(lambda i, rows: norm_back(acc[pl.ds(rows, BLOCK), :], 0, 0, rows, dzb))
 
@@ -1125,7 +1120,6 @@
     pump(*sum_self.both(sum_self.stage2))
     attend_back(0, qkv1, 0, (3, 6))
     norm_step(2)
-    pump(*[one.middle for one in quarters])
 
     key_ids = [new_id() for _ in range(2)]
 
@@ -1174,6 +1168,7 @@
         )
 
     pump(*sum_self.both(sum_self.stage3))
+    quarter_grads(t)
 
     pl.semaphore_wait(credit.at[2], 1)
     core_sums = [(a, n, new_id()) for a in range(2) for n in range(3)]
@@ -1206,6 +1201,7 @@
         yb[BLOCK:, :] = (res[BLOCK:, :] + dhk_recv[1].astype(F32) + own_part).astype(BF16)
 
     dx_begin, dx_close = return_row(dx_out)
+    pump(*[one.collect for one in quarters])
 
     for a, n, ident in core_sums:
         arrive(core_slot(a, n), ident)
@@ -1213,9 +1209,7 @@
     pl.semaphore_wait(credit.at[0], 2)
     sum_cross.start_all()
     norm_step(4)
-    quarter_grads(t)
     pump(
-        *[one.collect for one in quarters],
         *sum_cross.both(sum_cross.stage2),
         *sum_self.both(sum_self.stage4),
         *[one.relay for one in quarters],

time: 307 us -> 303 us (0.987)
    pallas_call x1, Pallas kernels: 293 us -> 290 us  [call_layer(): pl.pallas_call(layer_kernel, name='cross_modality_layer', out_shape=(jax....]
where the time goes in v2:
time: 303 us
  Pallas kernels  299 us (99%)
    pallas_call x1, Pallas kernels, call_layer(): pl.pallas_call(layer_kernel, name='cross_modality_layer', out_shape=(jax....  290 us
    pallas_call x1, Pallas kernels, call_results(): pl.pallas_call(results_kernel, name='results', out_shape=tuple((out(shape...  9.32 us

profile of v2, /device:TPU:0, one launch (start us, length us, event | category | flops | bytes accessed | tf_op | source)
XLA Modules:
  0.0 303.2 jit_solution(5934103967089471293)
XLA Ops:
  0.7 0.1 pad.2.clone
  0.8 0.1 pad.8.clone
  0.8 0.7 broadcast_in_dim.3
  1.6 0.1 reshape.23
  1.7 0.7 fusion.1
  2.5 0.1 stack.19
  2.5 0.6 convert_element_type.3.codes_in
  3.1 289.9 %cross_modality_layer.1 = (bf16[2,192,768]{2,1,0:T(8,128)(2,1)}, bf16[2,192,768]{2,1,0:T(8,128)(2,1)}, bf16[4,192,768]{2,1,0:T(8,128)(2,1)}, bf16[2,4,192,768]{3...) custom-call(bf16[2,192,768]{2,1,0:T(8,128)(2,1)} %x_in.1, ...), custom_call_target="tpu_custom_call" | custom-call | tf_op jit(solution)/shard_map/cross_modality_layer/pallas_call | solution.py:1254
  293.0 0.0 copy-start
  293.0 9.3 %results.1 = (f32[2,192,768]{2,1,0:T(8,128)}, f32[3,192,768]{2,1,0:T(8,128)}, f32[192,768]{1,0:T(8,128)}, f32[2,3,192,768]{3,2,1,0:T(8,128)}, f32[2,192,768]{2,1...) custom-call(bf16[4,192,768]{2,1,0:T(8,128)(2,1)} %get-tuple-element.27.cross, ...), custom_call_target="tpu_custom_call" | custom-call | tf_op jit(solution)/shard_map/results/pallas_call | solution.py:1391
  302.3 0.0 copy-done
  302.3 0.8 copy.24
  (10 shorter events, 0.0 us)
Async XLA Ops:
  293.0 9.3 %copy-start = (bf16[2,192,768]{2,1,0:T(8,128)(2,1)S(1)}, bf16[2,192,768]{2,1,0:T(8,128)(2,1)}, u32[]{:S(2)}) copy-start(bf16[2,192,768]{2,1,0:T(8,128)(2,1)} %get-tuple-element.55) | copy-start | bytes 1769476
